TPU v7x, 32 devices: a whole 2x2x4 slice. The times are simulated.
32 devices in a mesh: pa: 4 (over x, core), pb: 8 (over z, y).
Axes of the slice: x: 2, y: 2, z: 4, core: 2. Of those that a mesh axis runs over, the one named last changes fastest.
Arguments:
- point_keys: bfloat16 [4096, 768], P(('pa', 'pb')), may hold values from -7 to 7
- point_values: bfloat16 [4096, 768], P(('pa', 'pb')), may hold values from -40 to 40
- out_grad: bfloat16 [4096, 768], P(('pa', 'pb')), may hold values from -512 to 512
- decoder_norm: float32 [12, 4096], P(None, ('pa', 'pb')), as said below
- latent_query: bfloat16 [1024, 768], P(('pa', 'pb')), may hold values from -4 to 4
- latent_out: bfloat16 [1024, 768], P(('pa', 'pb')), may hold values from -5 to 5
- encoder_norm: float32 [12, 1024], replicated, as said below
Outputs:
- keys_grad: bfloat16 [4096, 768], P(('pa', 'pb'))
- values_grad: bfloat16 [4096, 768], P(('pa', 'pb'))
- latent_grad: float32 [1024, 768], P(('pa', 'pb'))
Inputs may be any that keep to these rules, and one draw needn't show every extreme that they name: `decoder_norm`: each entry lies between log(1024) - 0.3 and log(1024) + 1.3. `encoder_norm`: each entry lies between log(4096) - 0.3 and log(4096) + 1.3.
All inputs are finite; a program needn't handle non-finite values.
Results may differ from a plain program's by a relative error of at most 0.004.
The roundings to bfloat16 on the way count: a program that leaves them out, or rounds other values in their place, can miss the bound.
Values may be sent and summed in bfloat16 or wider, within the bound.
No kernel may reach another device: no remote copies, remote signals or barrier semaphores. Data moves between devices by JAX's collectives and lax.ppermute only.
A program may use at most 64 MiB of HBM per device.

v0:
```python
import jax
import jax.numpy as jnp
from jax import lax
from jax.sharding import PartitionSpec as P

HEADS = 12
HEAD_DIM = 64


def column(block, current):
    return lax.dynamic_slice_in_dim(block, current * HEAD_DIM, HEAD_DIM, 1)


def put_head(total, piece, current):
    return lax.dynamic_update_slice_in_dim(total, piece, current * HEAD_DIM, 1)


def add_head(total, piece, current):
    return put_head(total, column(total, current) + piece, current)


def across(left, right):
    return lax.dot_general(
        left, right, (((1,), (1,)), ((), ())), preferred_element_type=jnp.float32
    )


def down_rows(left, right):
    return lax.dot_general(
        left, right, (((0,), (0,)), ((), ())), preferred_element_type=jnp.float32
    )


def shards(
    point_keys, point_values, out_grad, decoder_norm, latent_query, latent_out, encoder_norm
):
    scale_factor = HEAD_DIM ** (-0.5)
    lat_all, out_all = (
        lax.all_gather(latent_query, ("pa", "pb"), axis=0, tiled=True),
        lax.all_gather(latent_out, ("pa", "pb"), axis=0, tiled=True),
    )
    point_rows = point_keys.shape[0]
    latent_rows = lat_all.shape[0]
    width = point_keys.shape[1]

    def encoder_row(current):
        return lax.dynamic_slice_in_dim(encoder_norm, current, 1, 0)

    def pass_one(current, state):
        mix_acc, query_acc, key_acc, weighted_acc = state
        key_head = column(point_keys, current)
        grad_head = column(out_grad, current)
        lat_head = column(lat_all, current)
        scores = across(key_head, lat_head) * scale_factor
        decoder_weights = jnp.exp(scores - lax.dynamic_slice_in_dim(decoder_norm, current, 1, 0).T)
        decoder_gradient = across(grad_head, column(out_all, current))
        row_total = jnp.sum(decoder_weights * decoder_gradient, axis=1, keepdims=True)
        decoder_scores_grad = (decoder_weights * (decoder_gradient - row_total)).astype(
            jnp.bfloat16
        )
        mix_acc = put_head(
            mix_acc, down_rows(decoder_weights.astype(jnp.bfloat16), grad_head), current
        )
        query_acc = put_head(
            query_acc, down_rows(decoder_scores_grad, key_head) * scale_factor, current
        )
        key_acc = put_head(
            key_acc,
            jnp.dot(decoder_scores_grad, lat_head, preferred_element_type=jnp.float32)
            * scale_factor,
            current,
        )
        return (mix_acc, query_acc, key_acc, weighted_acc)

    weighted_blank = jnp.zeros((1, 1), jnp.float32)
    latent_blank = jnp.zeros((latent_rows, width), jnp.float32)
    begin = (
        latent_blank,
        latent_blank,
        jnp.zeros((point_rows, width), jnp.float32),
        weighted_blank,
    )
    mix_acc, query_acc, key_acc, weighted_acc = lax.fori_loop(0, HEADS, pass_one, begin)
    mix_grad = lax.psum(mix_acc, ("pa", "pb"))
    mixing_portion = mix_grad.astype(jnp.bfloat16)

    def pass_two(current, state):
        partial_rows, value_acc = state
        scores = across(column(point_keys, current), column(lat_all, current)) * scale_factor
        encoder_portion = jnp.exp(scores - encoder_row(current)).astype(jnp.bfloat16)
        mix_head = column(mixing_portion, current)
        encoder_gradient = across(column(point_values, current), mix_head)
        sums = jnp.sum(encoder_portion.astype(jnp.float32) * encoder_gradient, axis=0)[None, :]
        partial_rows = lax.dynamic_update_slice_in_dim(partial_rows, sums, current, 0)
        value_acc = put_head(
            value_acc,
            jnp.dot(encoder_portion, mix_head, preferred_element_type=jnp.float32),
            current,
        )
        return (partial_rows, value_acc)

    partial_rows, value_acc = lax.fori_loop(
        0,
        HEADS,
        pass_two,
        (jnp.zeros((HEADS, latent_rows), jnp.float32), jnp.zeros((point_rows, width), jnp.float32)),
    )
    column_total = lax.psum(partial_rows, ("pa", "pb"))

    def pass_three(current, state):
        query_acc, key_acc, value_acc = state
        key_head = column(point_keys, current)
        lat_head = column(lat_all, current)
        mix_head = column(mixing_portion, current)
        scores = across(key_head, lat_head) * scale_factor
        encoder = jnp.exp(scores - encoder_row(current))
        encoder_gradient = across(column(point_values, current), mix_head)
        encoder_scores_grad = (
            encoder * (encoder_gradient - lax.dynamic_slice_in_dim(column_total, current, 1, 0))
        ).astype(jnp.bfloat16)
        query_acc = add_head(
            query_acc, down_rows(encoder_scores_grad, key_head) * scale_factor, current
        )
        key_acc = add_head(
            key_acc,
            jnp.dot(encoder_scores_grad, lat_head, preferred_element_type=jnp.float32)
            * scale_factor,
            current,
        )
        return (query_acc, key_acc, value_acc)

    query_acc, key_acc, value_acc = lax.fori_loop(
        0, HEADS, pass_three, (query_acc, key_acc, value_acc)
    )
    latent_grad = lax.psum_scatter(query_acc, ("pa", "pb"), scatter_dimension=0, tiled=True)
    return (key_acc.astype(jnp.bfloat16), value_acc.astype(jnp.bfloat16), latent_grad)


def solution(mesh):
    in_specs = (
        P(("pa", "pb"), None),
        P(("pa", "pb"), None),
        P(("pa", "pb"), None),
        P(None, ("pa", "pb")),
        P(("pa", "pb"), None),
        P(("pa", "pb"), None),
        P(),
    )
    out_specs = (P(("pa", "pb"), None), P(("pa", "pb"), None), P(("pa", "pb"), None))
    return jax.shard_map(shards, mesh=mesh, in_specs=in_specs, out_specs=out_specs, check_vma=False)
```

profile of v0, /device:TPU:0, one launch (start us, length us, event | category | flops | bytes accessed | tf_op | source)
XLA Modules:
  0.0 576.5 jit_solution(12292148037386380637)
XLA Ops:
  9.4 59.3 %all-gather.3.cloned.1.call-done = bf16[1024,768]{1,0:T(8,128)(2,1)} async-done(((bf16[32,768]{1,0:T(8,128)(2,1)}), bf16[1024,768]{1,0:T(8,128)(2,1)}) %all-gather.3.cloned.1.call-update) | async-done | bytes 1572880 | tf_op jit(solution)/shard_map/all_gather | solution.py:39
  68.7 56.9 %all-gather.5.cloned.1.call-done = bf16[1024,768]{1,0:T(8,128)(2,1)} async-done(((bf16[32,768]{1,0:T(8,128)(2,1)}), bf16[1024,768]{1,0:T(8,128)(2,1)}) %all-gather.5.cloned.1.call-update) | async-done | bytes 1572880 | tf_op jit(solution)/shard_map/all_gather | solution.py:40
  125.5 2.0 broadcast_in_dim.16
  127.6 2.1 broadcast_in_dim.16.clone
  129.7 86.6 %while.47 = (s32[]{:T(128)}, f32[1024,768]{0,1:T(8,128)}, f32[1024,768]{0,1:T(8,128)}, f32[128,768]{0,1:T(8,128)S(1)}, bf16[128,768]{1,0:T(8,128)(2,1)}, /*index...) while((s32[]{:T(128)}, f32[1024,768]{0,1:T(8,128)}, ...), condition=%wide.region_2.0_spmd, body=%wide.region_0.0_spmd.sunk | while | flops 85008256 | bytes 5414575 | solution.py:83
  216.3 3.6 copy.10
  219.9 76.8 %all-reduce.1 = bf16[1024,768]{1,0:T(8,128)(2,1)S(1)} all-reduce(f32[1024,768]{1,0:T(8,128)} %copy.10), channel_id=1, replica_groups=mesh['pa'=4,'pb'=8] {'pa','pb'}, use_global_device_ids=true, to_apply=%region_3.0 | all-reduce | flops 786432 | bytes 4718592 | tf_op jit(solution)/shard_map/psum | solution.py:84
  296.7 64.0 %while.48 = (s32[]{:T(128)}, f32[12,1024]{1,0:T(8,128)}, bf16[128,768]{0,1:T(8,128)(2,1)}, bf16[128,768]{1,0:T(8,128)(2,1)}, bf16[1024,768]{1,0:T(8,128)(2,1)S(1...) while((s32[]{:T(128)}, f32[12,1024]{1,0:T(8,128)}, ...), condition=%wide.region_6.0_spmd, body=%wide.region_4.0_spmd.sunk | while | flops 51117060 | bytes 1698987 | solution.py:102
  360.7 39.1 %psum.15 = f32[12,1024]{1,0:T(8,128)} all-reduce(f32[12,1024]{1,0:T(8,128)} %get-tuple-element.457), channel_id=1, replica_groups=mesh['pa'=4,'pb'=8] {'pa','pb'}, use_global_device_ids=true, to_apply=%region_7.0 | all-reduce | flops 12288 | bytes 98304 | tf_op jit(solution)/shard_map/psum | solution.py:108
  399.8 64.4 %while.49 = (s32[]{:T(128)}, f32[1024,768]{0,1:T(8,128)}, f32[128,768]{0,1:T(8,128)S(1)}, bf16[128,768]{1,0:T(8,128)(2,1)}, bf16[1024,768]{1,0:T(8,128)(2,1)S(1)...) while((s32[]{:T(128)}, f32[1024,768]{0,1:T(8,128)}, ...), condition=%wide.region_9.0_spmd, body=%wide.region_8.0_spmd.sunk | while | flops 67911680 | bytes 3338415 | solution.py:132
  402.8 2.0 fusion.114
  408.1 2.0 fusion.114
  413.5 2.0 fusion.114
  418.8 2.0 fusion.114
  424.2 2.0 fusion.114
  429.5 2.0 fusion.114
  434.9 2.0 fusion.114
  440.3 2.0 fusion.114
  445.6 2.0 fusion.114
  451.0 2.0 fusion.114
  456.4 2.0 fusion.114
  461.8 2.0 fusion.114
  464.1 3.5 copy.13
  469.4 100.6 %reduce-scatter.2.cloned.1.call-done = f32[32,768]{1,0:T(8,128)} async-done(((f32[1024,768]{1,0:T(8,128)}), f32[32,768]{1,0:T(8,128)}) %reduce-scatter.2.cloned.1.call-update) | async-done | bytes 98320 | tf_op jit(solution)/shard_map/reduce_scatter | solution.py:135
  (207 shorter events, 193.8 us)
Async XLA Ops:
  7.2 61.5 %all-gather.3.cloned.1.call-start = ((), (), s32[]{:S(2)}) async-start(), calls=%async_computation.1 | async-start | bytes 1622016 | tf_op jit(solution)/shard_map/all_gather | solution.py:39
  7.9 117.6 %all-gather.5.cloned.1.call-start = ((), (), s32[]{:S(2)}) async-start(), calls=%async_computation.2 | async-start | bytes 1622016 | tf_op jit(solution)/shard_map/all_gather | solution.py:40
  8.6 561.4 %reduce-scatter.2.cloned.1.call-start = ((), (), s32[]{:S(2)}) async-start(), calls=%async_computation.3 | async-start | bytes 3244032 | tf_op jit(solution)/shard_map/reduce_scatter | solution.py:135
  68.7 61.0 %copy-start = (bf16[1024,768]{1,0:T(8,128)(2,1)S(1)}, bf16[1024,768]{1,0:T(8,128)(2,1)}, u32[]{:S(2)}) copy-start(bf16[1024,768]{1,0:T(8,128)(2,1)} %all-gather.3.cloned.1.call-done) | copy-start | bytes 4718596
  467.7 0.9 copy-start.1
Sparse Core Ops, SparseCore 0:
  10.9 57.7 all-gather.2
  71.6 53.9 all-gather.4
  467.8 102.1 reduce-scatter.1
where the time goes:
time: 586 us; the launch traced here: 577 us
  waiting for transfers between devices  218 us (37%)
  matrix products  168 us (29%)
  blocking collectives  116 us (20%)
  local copies, waits for them, and re-layouts  56.8 us (10%)
  between operations  13.8 us (2%)
    reduce_scatter x1, waiting for transfers between devices, shards(): lax.psum_scatter(query_acc, ('pa', 'pb'), scatter_dimension=0, tiled=True)  101 us
    dot_general x72, matrix products, across(): lax.dot_general(left, right, (((1,), (1,)), ((), ())), preferred_element_...  81.6 us
    psum x1, blocking collectives, shards(): mix_grad = lax.psum(mix_acc, ('pa', 'pb'))  76.8 us
    dot_general x36, matrix products, down_rows(): lax.dot_general(left, right, (((0,), (0,)), ((), ())), preferred_element_...  66.1 us
    all_gather x1, waiting for transfers between devices, shards(): lax.all_gather(latent_query, ('pa', 'pb'), axis=0, tiled=True)  59.3 us
    all_gather x1, waiting for transfers between devices, shards(): lax.all_gather(latent_out, ('pa', 'pb'), axis=0, tiled=True)  56.9 us
    psum x1, blocking collectives, shards(): column_total = lax.psum(partial_rows, ('pa', 'pb'))  39.1 us
    dynamic_slice x24, local copies, waits for them, and re-layouts, encoder_row(): return lax.dynamic_slice_in_dim(encoder_norm, current, 1, 0)  18.6 us
  transfers between devices with their start and end apart: 3, of which 3 were waited for; matrix products, arithmetic and copies ran while one was open for 0% of the time, Pallas kernels for 0%

commit v1 on v0

--- a/solution.py
+++ b/solution.py
@@ -81,7 +81,7 @@
         weighted_blank,
     )
     mix_acc, query_acc, key_acc, weighted_acc = lax.fori_loop(0, HEADS, pass_one, begin)
-    mix_grad = lax.psum(mix_acc, ("pa", "pb"))
+    mix_grad = lax.psum(lax.psum(mix_acc, "pb"), "pa")
     mixing_portion = mix_grad.astype(jnp.bfloat16)
 
     def pass_two(current, state):

time: 586 us -> 702 us (1.20)
  waiting for transfers between devices: 218 us -> 346 us
  blocking collectives: 116 us -> 98.9 us
    psum x0 -> x1, waiting for transfers between devices: none -> 127 us  [shards(): mix_grad = lax.psum(lax.psum(mix_acc, 'pb'), 'pa')]
    psum x1, blocking collectives: 76.8 us -> 58.8 us  [shards(): mix_grad = lax.psum(lax.psum(mix_acc, 'pb'), 'pa')]
    dot_general x12, matrix products: 4.43 us -> 15.8 us  [pass_one(): jnp.dot(decoder_scores_grad, lat_head, preferred_element_type=jnp.float32)]
    dot_general x36, matrix products: 66.1 us -> 57.7 us  [down_rows(): lax.dot_general(left, right, (((0,), (0,)), ((), ())), preferred_element_...]
  transfers between devices with their start and end apart: 3 -> 4, of which waited for: 3 -> 4; matrix products, arithmetic and copies ran while one was open for 0% -> 0% of each run, Pallas kernels for 0% -> 0%
where the time goes in v1:
time: 702 us; the launch traced here: 693 us
  waiting for transfers between devices  346 us (49%)
  matrix products  174 us (25%)
  blocking collectives  98.9 us (14%)
  local copies, waits for them, and re-layouts  56.3 us (8%)
  between operations  13.8 us (2%)
    psum x1, waiting for transfers between devices, shards(): mix_grad = lax.psum(lax.psum(mix_acc, 'pb'), 'pa')  127 us
    reduce_scatter x1, waiting for transfers between devices, shards(): lax.psum_scatter(query_acc, ('pa', 'pb'), scatter_dimension=0, tiled=True)  101 us
    dot_general x72, matrix products, across(): lax.dot_general(left, right, (((1,), (1,)), ((), ())), preferred_element_...  84.2 us
    all_gather x1, waiting for transfers between devices, shards(): lax.all_gather(latent_query, ('pa', 'pb'), axis=0, tiled=True)  60 us
    psum x1, blocking collectives, shards(): mix_grad = lax.psum(lax.psum(mix_acc, 'pb'), 'pa')  58.8 us
    dot_general x36, matrix products, down_rows(): lax.dot_general(left, right, (((0,), (0,)), ((), ())), preferred_element_...  57.7 us
    all_gather x1, waiting for transfers between devices, shards(): lax.all_gather(latent_out, ('pa', 'pb'), axis=0, tiled=True)  56.9 us
    psum x1, blocking collectives, shards(): column_total = lax.psum(partial_rows, ('pa', 'pb'))  40.1 us
  transfers between devices with their start and end apart: 4, of which 4 were waited for; matrix products, arithmetic and copies ran while one was open for 0% of the time, Pallas kernels for 0%

profile of v1, /device:TPU:0, one launch (start us, length us, event | category | flops | bytes accessed | tf_op | source)
XLA Modules:
  0.0 692.7 jit_solution(8703374157869304728)
XLA Ops:
  8.7 60.0 %all-gather.3.cloned.1.call-done = bf16[1024,768]{1,0:T(8,128)(2,1)} async-done(((bf16[32,768]{1,0:T(8,128)(2,1)}), bf16[1024,768]{1,0:T(8,128)(2,1)}) %all-gather.3.cloned.1.call-update) | async-done | bytes 1572880 | tf_op jit(solution)/shard_map/all_gather | solution.py:39
  68.7 56.9 %all-gather.5.cloned.1.call-done = bf16[1024,768]{1,0:T(8,128)(2,1)} async-done(((bf16[32,768]{1,0:T(8,128)(2,1)}), bf16[1024,768]{1,0:T(8,128)(2,1)}) %all-gather.5.cloned.1.call-update) | async-done | bytes 1572880 | tf_op jit(solution)/shard_map/all_gather | solution.py:40
  125.5 2.1 broadcast_in_dim.16
  128.1 92.3 %while.47 = (s32[]{:T(128)}, f32[1024,768]{0,1:T(8,128)}, f32[1024,768]{0,1:T(8,128)S(1)}, f32[128,768]{0,1:T(8,128)S(1)}, bf16[128,768]{1,0:T(8,128)(2,1)}, /*i...) while((s32[]{:T(128)}, f32[1024,768]{0,1:T(8,128)}, ...), condition=%wide.region_2.0_spmd, body=%wide.region_0.0_spmd.sunk | while | flops 85008256 | bytes 5414575 | solution.py:83
  220.4 4.7 copy.10
  225.9 127.1 %all-reduce.3.cloned.1.call-done = f32[1024,768]{1,0:T(8,128)} async-done(((f32[1024,768]{1,0:T(8,128)}), f32[1024,768]{1,0:T(8,128)}) %all-reduce.3.cloned.1.call-update) | async-done | bytes 3145744 | tf_op jit(solution)/shard_map/psum | solution.py:84
  352.9 58.8 %all-reduce.4 = bf16[1024,768]{1,0:T(8,128)(2,1)S(1)} all-reduce(f32[1024,768]{1,0:T(8,128)} %all-reduce.3.cloned.1.call-done), channel_id=1, replica_groups=mesh['pa'=4,'pb'=8] {'pa'}, use_global_device_ids=true, to_apply=%region_4.0 | all-reduce | flops 786432 | bytes 4718592 | tf_op jit(solution)/shard_map/psum | solution.py:84
  411.7 64.0 %while.48 = (s32[]{:T(128)}, f32[12,1024]{1,0:T(8,128)}, bf16[128,768]{0,1:T(8,128)(2,1)}, bf16[128,768]{1,0:T(8,128)(2,1)}, bf16[1024,768]{1,0:T(8,128)(2,1)S(1...) while((s32[]{:T(128)}, f32[12,1024]{1,0:T(8,128)}, ...), condition=%wide.region_7.0_spmd, body=%wide.region_5.0_spmd.sunk | while | flops 51117060 | bytes 1698987 | solution.py:102
  475.7 40.1 %psum.23 = f32[12,1024]{1,0:T(8,128)} all-reduce(f32[12,1024]{1,0:T(8,128)} %get-tuple-element.457), channel_id=1, replica_groups=mesh['pa'=4,'pb'=8] {'pa','pb'}, use_global_device_ids=true, to_apply=%region_8.0 | all-reduce | flops 12288 | bytes 98304 | tf_op jit(solution)/shard_map/psum | solution.py:108
  515.8 64.4 %while.49 = (s32[]{:T(128)}, f32[1024,768]{0,1:T(8,128)}, f32[128,768]{0,1:T(8,128)S(1)}, bf16[128,768]{1,0:T(8,128)(2,1)}, bf16[1024,768]{1,0:T(8,128)(2,1)S(1)...) while((s32[]{:T(128)}, f32[1024,768]{0,1:T(8,128)}, ...), condition=%wide.region_10.0_spmd, body=%wide.region_9.0_spmd.sunk | while | flops 67911680 | bytes 3338415 | solution.py:132
  518.8 2.0 fusion.114
  524.1 2.0 fusion.114
  529.5 2.0 fusion.114
  534.8 2.0 fusion.114
  540.2 2.0 fusion.114
  545.6 2.0 fusion.114
  550.9 2.0 fusion.114
  556.3 2.0 fusion.114
  561.6 2.0 fusion.114
  567.0 2.0 fusion.114
  572.4 2.0 fusion.114
  577.8 2.0 fusion.114
  580.2 3.6 copy.13
  585.5 100.7 %reduce-scatter.2.cloned.1.call-done = f32[32,768]{1,0:T(8,128)} async-done(((f32[1024,768]{1,0:T(8,128)}), f32[32,768]{1,0:T(8,128)}) %reduce-scatter.2.cloned.1.call-update) | async-done | bytes 98320 | tf_op jit(solution)/shard_map/reduce_scatter | solution.py:135
  (212 shorter events, 199.9 us)
Async XLA Ops:
  7.2 61.5 %all-gather.3.cloned.1.call-start = ((), (), s32[]{:S(2)}) async-start(), calls=%async_computation.1 | async-start | bytes 1622016 | tf_op jit(solution)/shard_map/all_gather | solution.py:39
  7.9 117.6 %all-gather.5.cloned.1.call-start = ((), (), s32[]{:S(2)}) async-start(), calls=%async_computation.2 | async-start | bytes 1622016 | tf_op jit(solution)/shard_map/all_gather | solution.py:40
  8.6 344.3 %all-reduce.3.cloned.1.call-start = ((), (), s32[]{:S(2)}) async-start(), calls=%async_computation.3 | async-start | bytes 6291456 | tf_op jit(solution)/shard_map/psum | solution.py:84
  220.4 4.7 copy-start
  225.1 186.6 %copy-start.1 = (bf16[1024,768]{1,0:T(8,128)(2,1)S(1)}, bf16[1024,768]{1,0:T(8,128)(2,1)}, u32[]{:S(2)}) copy-start(bf16[1024,768]{1,0:T(8,128)(2,1)} %get-tuple-element.804) | copy-start | bytes 4718596
  225.1 461.0 %reduce-scatter.2.cloned.1.call-start = ((), (), s32[]{:S(2)}) async-start(), calls=%async_computation.4 | async-start | bytes 3244032 | tf_op jit(solution)/shard_map/reduce_scatter | solution.py:135
  583.7 0.9 copy-start.2
Sparse Core Ops, SparseCore 0:
  10.9 57.7 all-gather.2
  71.6 53.9 all-gather.4
  225.2 127.6 all-reduce.2
  583.9 102.2 reduce-scatter.1
